TPU v7x, 512 devices: a whole 4x4x16 slice. The times are simulated.
512 devices in a mesh: lat: 16 (over x, y_lo, core), lon: 32 (over y_hi, z).
Axes of the slice: x: 4, y: 4 (y_hi: 2, y_lo: 2; y = y_hi * 2 + y_lo), z: 16, core: 2. Of those that a mesh axis runs over, the one named last changes fastest.
Arguments:
- features: bfloat16 [64, 1024, 256], P('lat', 'lon'), may hold values from -6 to 6
- cotangent: bfloat16 [64, 1024, 256], P('lat', 'lon'), may hold values from -6 to 6
- weight: bfloat16 [4, 256, 256], replicated, may hold values from -0.1875 to 0.1875
- filter_taps: bfloat16 [64, 4, 5, 64], P('lat'), may hold values from -6 to 6
- lat_ext: int32 [64], P('lat'), may hold values from 1 to 3, as said below
- lon_count: int32 [64], P('lat'), may hold values from 1 to 32, as said below
Outputs:
- output: bfloat16 [64, 1024, 256], P('lat', 'lon')
- field_grad: bfloat16 [64, 1024, 256], P('lat', 'lon')
- weight_grad: float32 [4, 256, 256], replicated
Inputs may be any that keep to these rules, and one draw needn't show every extreme that they name: `lat_ext`: a row uses the latitude offsets whose magnitude is below its entry. `lon_count`: a row uses the longitude offsets whose magnitude is below its entry.
All inputs are finite; a program needn't handle non-finite values.
Results may differ from a plain program's by a relative error of at most 0.006.
Values may be sent and summed in bfloat16 or wider, within the bound.
A program may use at most 64 MiB of HBM per device.

v0:
```python
import math
import jax
import jax.numpy as jnp
from jax import lax
from jax.sharding import PartitionSpec as P


def extended(cells, sides, width, closed):
    for axis, dim in sides:
        count = lax.axis_size(axis)
        ends = count if closed else count - 1
        head = lax.slice_in_dim(cells, 0, width, axis=dim)
        tail = lax.slice_in_dim(cells, cells.shape[dim] - width, cells.shape[dim], axis=dim)
        cells = jnp.concatenate(
            [
                lax.ppermute(tail, axis, [(i, (i + 1) % count) for i in range(ends)]),
                cells,
                lax.ppermute(head, axis, [((i + 1) % count, i) for i in range(ends)]),
            ],
            axis=dim,
        )
    return cells


def make_filters(filter_taps, lat_ext, lon_count):
    lat_reach = filter_taps.shape[2] // 2
    half_width = filter_taps.shape[3] // 2
    lat_dist = jnp.abs(jnp.arange(filter_taps.shape[2], dtype=jnp.int32) - lat_reach)
    lon_dist = jnp.abs(jnp.arange(filter_taps.shape[3], dtype=jnp.int32) - half_width)
    support = (lat_dist[None, :, None] < lat_ext[:, None, None]) & (
        lon_dist[None, None, :] < lon_count[:, None, None]
    )
    support_size = ((2 * lat_ext - 1) * (2 * lon_count - 1)).astype(jnp.float32)
    row_scale = lax.rsqrt(support_size)
    masked = (
        filter_taps.astype(jnp.float32)
        * support[:, None].astype(jnp.float32)
        * row_scale[:, None, None, None]
    )
    return masked.astype(jnp.bfloat16)


def forward_taps(row_taps, lon_width):
    leading = row_taps.shape[:-1]
    return jnp.concatenate(
        [row_taps, jnp.zeros(leading + (lon_width + 1,), row_taps.dtype)], axis=-1
    )


def reverse_taps(row_taps, lon_width):
    leading = row_taps.shape[:-1]
    return jnp.concatenate(
        [
            jnp.zeros(leading + (1,), row_taps.dtype),
            row_taps[..., ::-1],
            jnp.zeros(leading + (lon_width,), row_taps.dtype),
        ],
        axis=-1,
    )


def band_matrix(padded, lon_width):
    leading = padded.shape[:-1]
    repeated = jnp.tile(padded, (1,) * len(leading) + (lon_width,))
    return repeated[..., : lon_width * 3 * lon_width].reshape(leading + (lon_width, 3 * lon_width))


def gather_adjoint(filter_rims, basis_rows, row_count, lon_width, channels, basis_count, lat_taps):
    last = lat_taps - 1
    diagonal = jnp.stack(
        [
            filter_rims[last - offset : last - offset + row_count, :, offset]
            for offset in range(lat_taps)
        ],
        axis=2,
    )
    banded = band_matrix(reverse_taps(diagonal, lon_width), lon_width)
    total_grad = jnp.zeros((row_count, lon_width, channels), jnp.float32)
    for basis_index in range(basis_count):
        grad_window = basis_rows(basis_index)
        patches = jnp.stack(
            [grad_window[last - offset : last - offset + row_count] for offset in range(lat_taps)],
            axis=1,
        )
        total_grad = total_grad + jnp.einsum(
            "oejn,oenc->ojc", banded[:, basis_index], patches, preferred_element_type=jnp.float32
        )
    return total_grad


def per_device(features, cotangent, weight, filter_taps, lat_ext, lon_count):
    row_count, lon_width, channels = features.shape
    basis_count = weight.shape[0]
    lat_taps = filter_taps.shape[2]
    lat_reach = lat_taps // 2
    filters = make_filters(filter_taps, lat_ext, lon_count)
    band_rows = extended(features, (("lat", 0),), lat_reach, False)
    window = extended(band_rows, (("lon", 1),), lon_width, True)
    banded_all = band_matrix(forward_taps(filters, lon_width), lon_width)
    patches = jnp.stack([window[offset : offset + row_count] for offset in range(lat_taps)], axis=1)
    basis_f32 = jnp.einsum(
        "okejm,oemc->ojkc", banded_all, patches, preferred_element_type=jnp.float32
    )
    basis_out = basis_f32.astype(jnp.bfloat16)
    flat_out = basis_out.reshape(row_count * lon_width, basis_count * channels)
    flat_weight = weight.reshape(basis_count * channels, channels)
    output = jnp.dot(flat_out, flat_weight, preferred_element_type=jnp.float32).astype(jnp.bfloat16)
    output = output.reshape(row_count, lon_width, channels)
    flat_cot = cotangent.reshape(row_count * lon_width, channels)
    partial_grad = lax.dot_general(
        flat_out, flat_cot, (((0,), (0,)), ((), ())), preferred_element_type=jnp.float32
    )
    total_cells = row_count * lax.axis_size("lat") * lon_width * lax.axis_size("lon")
    summed_grad = lax.psum(partial_grad, ("lat", "lon"))
    weight_grad = (summed_grad * (1.0 / math.sqrt(total_cells))).reshape(
        basis_count, channels, channels
    )
    filter_rims = extended(filters, (("lat", 0),), lat_reach, False)

    def received_rows(basis_index):
        own_grad = lax.dot_general(
            flat_cot,
            weight[basis_index],
            (((1,), (1,)), ((), ())),
            preferred_element_type=jnp.float32,
        ).astype(jnp.bfloat16)
        own_grad = own_grad.reshape(row_count, lon_width, channels)
        grad_band = extended(own_grad, (("lat", 0),), lat_reach, False)
        return extended(grad_band, (("lon", 1),), lon_width, True)

    field_grad = gather_adjoint(
        filter_rims, received_rows, row_count, lon_width, channels, basis_count, lat_taps
    ).astype(jnp.bfloat16)
    return (output, field_grad, weight_grad)


def solution(mesh):
    in_specs = (
        P("lat", "lon", None),
        P("lat", "lon", None),
        P(),
        P("lat", None, None, None),
        P("lat"),
        P("lat"),
    )
    out_specs = (P("lat", "lon", None), P("lat", "lon", None), P())
    return jax.shard_map(
        per_device, mesh=mesh, in_specs=in_specs, out_specs=out_specs, check_vma=False
    )
```

profile of v0, /device:TPU:1, one launch (start us, length us, event | category | flops | bytes accessed | tf_op | source)
XLA Modules:
  0.0 597.4 jit_solution(2804473898359303226)
XLA Ops:
  8.0 1.1 convolution_convert_fusion.4
  9.7 4.6 collective-permute-start.6
  14.3 5.5 collective-permute-start.7
  22.8 1.9 collective-permute-start.4
  24.8 3.6 collective-permute-start.5
  29.3 1.9 collective-permute-start.10
  33.9 1.8 tile.9
  36.4 2.4 collective-permute-start.11
  38.9 3.2 collective-permute-start.14
  42.4 1.8 tile.21
  45.1 1.9 collective-permute-start.15
  47.0 3.6 collective-permute-start.18
  50.7 1.9 collective-permute-start.19
  52.7 3.6 collective-permute-start
  56.4 1.0 collective-permute-done
  57.3 1.9 collective-permute-start.1
  59.3 1.9 collective-permute-start.8
  61.2 10.9 %collective-permute-start.9 = (bf16[8,32,256]{2,1,0:T(8,128)(2,1)S(1)}, bf16[8,32,256]{2,1,0:T(8,128)(2,1)S(1)}, u32[]{:S(2)}, u32[]{:S(2)}) collective-permute-start(bf16[8,32,256]{2,1,0:T(8,128)(2,1)S(1)} %pad_maximum_fusion.5), channel_id=1, source_target_pairs={{1,0},{2,1},{3,2},{4,3},{5,4},{6,5},{7,6},{8,7},{9,8},{10,9},{11,1... | collective-permute-start | bytes 393224 | tf_op jit(solution)/shard_map/ppermute | solution.py:18
  72.2 1.9 collective-permute-start.12
  74.1 7.0 %collective-permute-start.13 = (bf16[8,32,256]{2,1,0:T(8,128)(2,1)S(1)}, bf16[8,32,256]{2,1,0:T(8,128)(2,1)S(1)}, u32[]{:S(2)}, u32[]{:S(2)}) collective-permute-start(bf16[8,32,256]{2,1,0:T(8,128)(2,1)S(1)} %pad_maximum_fusion.6), channel_id=1, source_target_pairs={{1,0},{2,1},{3,2},{4,3},{5,4},{6,5},{7,6},{8,7},{9,8},{10,9},{11,1... | collective-permute-start | bytes 393224 | tf_op jit(solution)/shard_map/ppermute | solution.py:18
  81.1 1.9 collective-permute-start.16
  83.1 7.0 %collective-permute-start.17 = (bf16[8,32,256]{2,1,0:T(8,128)(2,1)S(1)}, bf16[8,32,256]{2,1,0:T(8,128)(2,1)S(1)}, u32[]{:S(2)}, u32[]{:S(2)}) collective-permute-start(bf16[8,32,256]{2,1,0:T(8,128)(2,1)S(1)} %pad_maximum_fusion.7), channel_id=1, source_target_pairs={{1,0},{2,1},{3,2},{4,3},{5,4},{6,5},{7,6},{8,7},{9,8},{10,9},{11,1... | collective-permute-start | bytes 393224 | tf_op jit(solution)/shard_map/ppermute | solution.py:18
  90.1 1.9 collective-permute-start.20
  92.1 7.0 %collective-permute-start.21 = (bf16[8,32,256]{2,1,0:T(8,128)(2,1)S(1)}, bf16[8,32,256]{2,1,0:T(8,128)(2,1)S(1)}, u32[]{:S(2)}, u32[]{:S(2)}) collective-permute-start(bf16[8,32,256]{2,1,0:T(8,128)(2,1)S(1)} %pad_maximum_fusion.8), channel_id=1, source_target_pairs={{1,0},{2,1},{3,2},{4,3},{5,4},{6,5},{7,6},{8,7},{9,8},{10,9},{11,1... | collective-permute-start | bytes 393224 | tf_op jit(solution)/shard_map/ppermute | solution.py:18
  99.1 1.9 collective-permute-start.2
  101.2 7.0 %collective-permute-start.3 = (bf16[8,32,256]{2,1,0:T(8,128)(2,1)S(1)}, bf16[8,32,256]{2,1,0:T(8,128)(2,1)S(1)}, u32[]{:S(2)}, u32[]{:S(2)}) collective-permute-start(bf16[8,32,256]{2,1,0:T(8,128)(2,1)S(1)} %constant_dynamic-update-slice_fusion), channel_id=1, source_target_pairs={{1,0},{2,1},{3,2},{4,3},{5,4},{6,5},{7,6},{8,7},{9,8},{10,9},{11,1... | collective-permute-start | bytes 393224 | tf_op jit(solution)/shard_map/ppermute | solution.py:18
  108.4 0.9 copy-done.4
  111.6 1.3 fusion.46
  112.9 0.9 convolution_convert_fusion
  115.7 1.0 fusion.5
  116.7 471.6 %all-reduce.3.cloned.1.call-done = f32[1024,256]{1,0:T(8,128)} async-done(((f32[1024,256]{1,0:T(8,128)}), f32[1024,256]{1,0:T(8,128)}) %all-reduce.3.cloned.1.call-update) | async-done | bytes 1048592 | tf_op jit(solution)/shard_map/psum | solution.py:114
  588.3 2.3 broadcast_multiply_fusion
  (122 shorter events, 14.5 us)
Async XLA Ops:
  7.2 21.2 %copy-start.1 = (bf16[4,256,256]{2,1,0:T(8,128)(2,1)S(1)}, bf16[4,256,256]{2,1,0:T(8,128)(2,1)}, u32[]{:S(2)}) copy-start(bf16[4,256,256]{2,1,0:T(8,128)(2,1)} %param.8) | copy-start | bytes 1572868
  7.2 581.1 %all-reduce.3.cloned.1.call-start = ((), (), s32[]{:S(2)}) async-start(), calls=%async_computation | async-start | bytes 2097152 | tf_op jit(solution)/shard_map/psum | solution.py:114
  9.7 35.1 %collective-permute-start.6 = (bf16[2,32,256]{2,1,0:T(8,128)(2,1)}, bf16[2,32,256]{2,1,0:T(8,128)(2,1)S(1)}, u32[]{:S(2)}, u32[]{:S(2)}) collective-permute-start(bf16[2,32,256]{2,1,0:T(8,128)(2,1)} %bitcast.19), channel_id=1, source_target_pairs={{0,32},{32,64},{64,96},{96,128},{128,160},{160,192},{192,224},{224... | collective-permute-start | bytes 98312 | tf_op jit(solution)/shard_map/ppermute | solution.py:16
  14.3 32.7 %collective-permute-start.7 = (bf16[2,32,256]{2,1,0:T(8,128)(2,1)}, bf16[2,32,256]{2,1,0:T(8,128)(2,1)S(1)}, u32[]{:S(2)}, u32[]{:S(2)}) collective-permute-start(bf16[2,32,256]{2,1,0:T(8,128)(2,1)} %bitcast.21), channel_id=1, source_target_pairs={{32,0},{64,32},{96,64},{128,96},{160,128},{192,160},{224,192},{256... | collective-permute-start | bytes 98312 | tf_op jit(solution)/shard_map/ppermute | solution.py:18
  22.8 13.5 %collective-permute-start.4 = (bf16[2,4,5,64]{3,1,2,0:T(4,128)(2,1)S(1)}, bf16[2,4,5,64]{3,1,2,0:T(4,128)(2,1)S(1)}, u32[]{:S(2)}, u32[]{:S(2)}) collective-permute-start(bf16[2,4,5,64]{3,1,2,0:T(4,128)(2,1)S(1)} %get-tuple-element.14), channel_id=1, source_target_pairs={{32,0},{64,32},{96,64},{128,96},{160,128},{192,160},{224,192},{256... | collective-permute-start | bytes 15368 | tf_op jit(solution)/shard_map/ppermute | solution.py:18
  24.8 14.1 %collective-permute-start.5 = (bf16[2,4,5,64]{3,1,2,0:T(4,128)(2,1)S(1)}, bf16[2,4,5,64]{3,1,2,0:T(4,128)(2,1)S(1)}, u32[]{:S(2)}, u32[]{:S(2)}) collective-permute-start(bf16[2,4,5,64]{3,1,2,0:T(4,128)(2,1)S(1)} %get-tuple-element.13), channel_id=1, source_target_pairs={{0,32},{32,64},{64,96},{96,128},{128,160},{160,192},{192,224},{224... | collective-permute-start | bytes 15368 | tf_op jit(solution)/shard_map/ppermute | solution.py:16
  29.3 21.5 %collective-permute-start.10 = (bf16[2,32,256]{2,1,0:T(8,128)(2,1)}, bf16[2,32,256]{2,1,0:T(8,128)(2,1)S(1)}, u32[]{:S(2)}, u32[]{:S(2)}) collective-permute-start(bf16[2,32,256]{2,1,0:T(8,128)(2,1)} %bitcast.35), channel_id=1, source_target_pairs={{0,32},{32,64},{64,96},{96,128},{128,160},{160,192},{192,224},{224... | collective-permute-start | bytes 98312 | tf_op jit(solution)/shard_map/ppermute | solution.py:16
  36.4 16.3 %collective-permute-start.11 = (bf16[2,32,256]{2,1,0:T(8,128)(2,1)}, bf16[2,32,256]{2,1,0:T(8,128)(2,1)S(1)}, u32[]{:S(2)}, u32[]{:S(2)}) collective-permute-start(bf16[2,32,256]{2,1,0:T(8,128)(2,1)} %bitcast.37), channel_id=1, source_target_pairs={{32,0},{64,32},{96,64},{128,96},{160,128},{192,160},{224,192},{256... | collective-permute-start | bytes 98312 | tf_op jit(solution)/shard_map/ppermute | solution.py:18
  38.9 20.4 %collective-permute-start.14 = (bf16[2,32,256]{2,1,0:T(8,128)(2,1)}, bf16[2,32,256]{2,1,0:T(8,128)(2,1)S(1)}, u32[]{:S(2)}, u32[]{:S(2)}) collective-permute-start(bf16[2,32,256]{2,1,0:T(8,128)(2,1)} %bitcast.51), channel_id=1, source_target_pairs={{0,32},{32,64},{64,96},{96,128},{128,160},{160,192},{192,224},{224... | collective-permute-start | bytes 98312 | tf_op jit(solution)/shard_map/ppermute | solution.py:16
  45.1 16.1 %collective-permute-start.15 = (bf16[2,32,256]{2,1,0:T(8,128)(2,1)S(1)}, bf16[2,32,256]{2,1,0:T(8,128)(2,1)S(1)}, u32[]{:S(2)}, u32[]{:S(2)}) collective-permute-start(bf16[2,32,256]{2,1,0:T(8,128)(2,1)S(1)} %bitcast.276), channel_id=1, source_target_pairs={{32,0},{64,32},{96,64},{128,96},{160,128},{192,160},{224,192},{256... | collective-permute-start | bytes 98312 | tf_op jit(solution)/shard_map/ppermute | solution.py:18
  47.0 27.1 %collective-permute-start.18 = (bf16[2,32,256]{2,1,0:T(8,128)(2,1)S(1)}, bf16[2,32,256]{2,1,0:T(8,128)(2,1)S(1)}, u32[]{:S(2)}, u32[]{:S(2)}) collective-permute-start(bf16[2,32,256]{2,1,0:T(8,128)(2,1)S(1)} %bitcast.275), channel_id=1, source_target_pairs={{0,32},{32,64},{64,96},{96,128},{128,160},{160,192},{192,224},{224... | collective-permute-start | bytes 98312 | tf_op jit(solution)/shard_map/ppermute | solution.py:16
  50.7 2.0 copy-start.11
  50.7 30.4 %collective-permute-start.19 = (bf16[2,32,256]{2,1,0:T(8,128)(2,1)S(1)}, bf16[2,32,256]{2,1,0:T(8,128)(2,1)S(1)}, u32[]{:S(2)}, u32[]{:S(2)}) collective-permute-start(bf16[2,32,256]{2,1,0:T(8,128)(2,1)S(1)} %bitcast.274), channel_id=1, source_target_pairs={{32,0},{64,32},{96,64},{128,96},{160,128},{192,160},{224,192},{256... | collective-permute-start | bytes 98312 | tf_op jit(solution)/shard_map/ppermute | solution.py:18
  52.7 4.7 collective-permute-start
  56.3 1.0 copy-start.9
  57.3 14.8 %collective-permute-start.1 = (bf16[2,32,256]{2,1,0:T(8,128)(2,1)S(1)}, bf16[2,32,256]{2,1,0:T(8,128)(2,1)S(1)}, u32[]{:S(2)}, u32[]{:S(2)}) collective-permute-start(bf16[2,32,256]{2,1,0:T(8,128)(2,1)S(1)} %copy-done.9), channel_id=1, source_target_pairs={{32,0},{64,32},{96,64},{128,96},{160,128},{192,160},{224,192},{256... | collective-permute-start | bytes 98312 | tf_op jit(solution)/shard_map/ppermute | solution.py:18
  59.3 23.8 %collective-permute-start.8 = (bf16[8,32,256]{2,1,0:T(8,128)(2,1)S(1)}, bf16[8,32,256]{2,1,0:T(8,128)(2,1)S(1)}, u32[]{:S(2)}, u32[]{:S(2)}) collective-permute-start(bf16[8,32,256]{2,1,0:T(8,128)(2,1)S(1)} %pad_maximum_fusion.5), channel_id=1, source_target_pairs={{0,1},{1,2},{2,3},{3,4},{4,5},{5,6},{6,7},{7,8},{8,9},{9,10},{10,1... | collective-permute-start | bytes 393224 | tf_op jit(solution)/shard_map/ppermute | solution.py:16
  61.2 28.8 %collective-permute-start.9 = (bf16[8,32,256]{2,1,0:T(8,128)(2,1)S(1)}, bf16[8,32,256]{2,1,0:T(8,128)(2,1)S(1)}, u32[]{:S(2)}, u32[]{:S(2)}) collective-permute-start(bf16[8,32,256]{2,1,0:T(8,128)(2,1)S(1)} %pad_maximum_fusion.5), channel_id=1, source_target_pairs={{1,0},{2,1},{3,2},{4,3},{5,4},{6,5},{7,6},{8,7},{9,8},{10,9},{11,1... | collective-permute-start | bytes 393224 | tf_op jit(solution)/shard_map/ppermute | solution.py:18
  72.2 20.0 %collective-permute-start.12 = (bf16[8,32,256]{2,1,0:T(8,128)(2,1)S(1)}, bf16[8,32,256]{2,1,0:T(8,128)(2,1)S(1)}, u32[]{:S(2)}, u32[]{:S(2)}) collective-permute-start(bf16[8,32,256]{2,1,0:T(8,128)(2,1)S(1)} %pad_maximum_fusion.6), channel_id=1, source_target_pairs={{0,1},{1,2},{2,3},{3,4},{4,5},{5,6},{6,7},{7,8},{8,9},{9,10},{10,1... | collective-permute-start | bytes 393224 | tf_op jit(solution)/shard_map/ppermute | solution.py:16
  74.1 25.0 %collective-permute-start.13 = (bf16[8,32,256]{2,1,0:T(8,128)(2,1)S(1)}, bf16[8,32,256]{2,1,0:T(8,128)(2,1)S(1)}, u32[]{:S(2)}, u32[]{:S(2)}) collective-permute-start(bf16[8,32,256]{2,1,0:T(8,128)(2,1)S(1)} %pad_maximum_fusion.6), channel_id=1, source_target_pairs={{1,0},{2,1},{3,2},{4,3},{5,4},{6,5},{7,6},{8,7},{9,8},{10,9},{11,1... | collective-permute-start | bytes 393224 | tf_op jit(solution)/shard_map/ppermute | solution.py:18
  81.1 20.1 %collective-permute-start.16 = (bf16[8,32,256]{2,1,0:T(8,128)(2,1)S(1)}, bf16[8,32,256]{2,1,0:T(8,128)(2,1)S(1)}, u32[]{:S(2)}, u32[]{:S(2)}) collective-permute-start(bf16[8,32,256]{2,1,0:T(8,128)(2,1)S(1)} %pad_maximum_fusion.7), channel_id=1, source_target_pairs={{0,1},{1,2},{2,3},{3,4},{4,5},{5,6},{6,7},{7,8},{8,9},{9,10},{10,1... | collective-permute-start | bytes 393224 | tf_op jit(solution)/shard_map/ppermute | solution.py:16
  83.1 25.2 %collective-permute-start.17 = (bf16[8,32,256]{2,1,0:T(8,128)(2,1)S(1)}, bf16[8,32,256]{2,1,0:T(8,128)(2,1)S(1)}, u32[]{:S(2)}, u32[]{:S(2)}) collective-permute-start(bf16[8,32,256]{2,1,0:T(8,128)(2,1)S(1)} %pad_maximum_fusion.7), channel_id=1, source_target_pairs={{1,0},{2,1},{3,2},{4,3},{5,4},{6,5},{7,6},{8,7},{9,8},{10,9},{11,1... | collective-permute-start | bytes 393224 | tf_op jit(solution)/shard_map/ppermute | solution.py:18
  90.1 18.4 %collective-permute-start.20 = (bf16[8,32,256]{2,1,0:T(8,128)(2,1)S(1)}, bf16[8,32,256]{2,1,0:T(8,128)(2,1)S(1)}, u32[]{:S(2)}, u32[]{:S(2)}) collective-permute-start(bf16[8,32,256]{2,1,0:T(8,128)(2,1)S(1)} %pad_maximum_fusion.8), channel_id=1, source_target_pairs={{0,1},{1,2},{2,3},{3,4},{4,5},{5,6},{6,7},{7,8},{8,9},{9,10},{10,1... | collective-permute-start | bytes 393224 | tf_op jit(solution)/shard_map/ppermute | solution.py:16
  92.1 17.2 %collective-permute-start.21 = (bf16[8,32,256]{2,1,0:T(8,128)(2,1)S(1)}, bf16[8,32,256]{2,1,0:T(8,128)(2,1)S(1)}, u32[]{:S(2)}, u32[]{:S(2)}) collective-permute-start(bf16[8,32,256]{2,1,0:T(8,128)(2,1)S(1)} %pad_maximum_fusion.8), channel_id=1, source_target_pairs={{1,0},{2,1},{3,2},{4,3},{5,4},{6,5},{7,6},{8,7},{9,8},{10,9},{11,1... | collective-permute-start | bytes 393224 | tf_op jit(solution)/shard_map/ppermute | solution.py:18
  99.1 10.6 %collective-permute-start.2 = (bf16[8,32,256]{2,1,0:T(8,128)(2,1)S(1)}, bf16[8,32,256]{2,1,0:T(8,128)(2,1)S(1)}, u32[]{:S(2)}, u32[]{:S(2)}) collective-permute-start(bf16[8,32,256]{2,1,0:T(8,128)(2,1)S(1)} %constant_dynamic-update-slice_fusion), channel_id=1, source_target_pairs={{0,1},{1,2},{2,3},{3,4},{4,5},{5,6},{6,7},{7,8},{8,9},{9,10},{10,1... | collective-permute-start | bytes 393224 | tf_op jit(solution)/shard_map/ppermute | solution.py:16
  101.2 7.0 %copy-start.2 = (bf16[4,5,96,256]{3,2,1,0:T(8,128)(2,1)}, bf16[4,5,96,256]{3,2,1,0:T(8,128)(2,1)S(1)}, u32[]{:S(2)}) copy-start(bf16[4,5,96,256]{3,2,1,0:T(8,128)(2,1)S(1)} %fusion.17) | copy-start | bytes 2949124
  101.2 9.6 %collective-permute-start.3 = (bf16[8,32,256]{2,1,0:T(8,128)(2,1)S(1)}, bf16[8,32,256]{2,1,0:T(8,128)(2,1)S(1)}, u32[]{:S(2)}, u32[]{:S(2)}) collective-permute-start(bf16[8,32,256]{2,1,0:T(8,128)(2,1)S(1)} %constant_dynamic-update-slice_fusion), channel_id=1, source_target_pairs={{1,0},{2,1},{3,2},{4,3},{5,4},{6,5},{7,6},{8,7},{9,8},{10,9},{11,1... | collective-permute-start | bytes 393224 | tf_op jit(solution)/shard_map/ppermute | solution.py:18
  108.4 0.9 copy-start.4
  109.5 0.9 copy-start.6
  112.9 1.2 copy-start.3
  113.8 1.3 copy-start.7
  114.1 1.3 copy-start.5
  (3 other events, 2.4 us)
Sparse Core Ops, SparseCore 0:
  113.0 475.2 all-reduce.2
where the time goes:
time: 598 us; the launch traced here: 597 us
  waiting for transfers between devices  473 us (79%)
  starting transfers between devices  84.5 us (14%)
  between operations  14.9 us (2%)
  local copies, waits for them, and re-layouts  12.9 us (2%)
  matrix products  6.08 us (1%)
    psum x1, waiting for transfers between devices, per_device(): summed_grad = lax.psum(partial_grad, ('lat', 'lon'))  472 us
    ppermute x11, starting transfers between devices, extended(): lax.ppermute(head, axis, [((i + 1) % count, i) for i in range(ends)])  54.3 us
    ppermute x11, starting transfers between devices, extended(): lax.ppermute(tail, axis, [(i, (i + 1) % count) for i in range(ends)])  30.2 us
  transfers between devices with their start and end apart: 23, of which 4 were waited for; matrix products, arithmetic and copies ran while one was open for 2% of the time, Pallas kernels for 0%

commit v1 on v0

--- a/solution.py
+++ b/solution.py
@@ -111,7 +111,7 @@
         flat_out, flat_cot, (((0,), (0,)), ((), ())), preferred_element_type=jnp.float32
     )
     total_cells = row_count * lax.axis_size("lat") * lon_width * lax.axis_size("lon")
-    summed_grad = lax.psum(partial_grad, ("lat", "lon"))
+    summed_grad = lax.psum(lax.psum(partial_grad, "lat"), "lon")
     weight_grad = (summed_grad * (1.0 / math.sqrt(total_cells))).reshape(
         basis_count, channels, channels
     )

time: 598 us -> 566 us (0.946)
  the two profiles are of different devices: /device:TPU:1 before, /device:TPU:2 now
where the time goes in v1:
time: 566 us; the launch traced here: 565 us
  waiting for transfers between devices  440 us (78%)
  starting transfers between devices  87.8 us (16%)
  between operations  14.9 us (3%)
  local copies, waits for them, and re-layouts  10.6 us (2%)
  matrix products  6.08 us (1%)
    psum x2, waiting for transfers between devices, per_device(): summed_grad = lax.psum(lax.psum(partial_grad, 'lat'), 'lon')  434 us
    ppermute x11, starting transfers between devices, extended(): lax.ppermute(head, axis, [((i + 1) % count, i) for i in range(ends)])  64 us
    ppermute x11, starting transfers between devices, extended(): lax.ppermute(tail, axis, [(i, (i + 1) % count) for i in range(ends)])  23.8 us
  transfers between devices with their start and end apart: 24, of which 5 were waited for; matrix products, arithmetic and copies ran while one was open for 3% of the time, Pallas kernels for 0%

profile of v1, /device:TPU:2, one launch (start us, length us, event | category | flops | bytes accessed | tf_op | source)
XLA Modules:
  0.0 565.5 jit_solution(13620671712382292068)
XLA Ops:
  8.0 1.1 convolution_convert_fusion.4
  9.1 1.9 collective-permute-start.6
  11.1 4.5 collective-permute-start.7
  18.7 1.9 collective-permute-start.4
  20.6 2.4 collective-permute-start.5
  23.2 2.2 collective-permute-start.10
  26.9 1.8 tile.9
  28.9 1.4 reshape.131
  30.2 4.2 collective-permute-start.11
  34.6 1.9 collective-permute-start.14
  36.8 1.8 tile.21
  39.4 4.5 collective-permute-start.15
  43.9 1.9 collective-permute-start.18
  45.9 4.5 collective-permute-start.19
  50.4 1.9 collective-permute-start
  52.4 4.2 collective-permute-done
  56.6 1.9 collective-permute-start.1
  58.5 3.8 collective-permute-start.8
  62.4 12.1 %collective-permute-start.9 = (bf16[8,32,256]{2,1,0:T(8,128)(2,1)S(1)}, bf16[8,32,256]{2,1,0:T(8,128)(2,1)S(1)}, u32[]{:S(2)}, u32[]{:S(2)}) collective-permute-start(bf16[8,32,256]{2,1,0:T(8,128)(2,1)S(1)} %pad_maximum_fusion.5), channel_id=1, source_target_pairs={{1,0},{2,1},{3,2},{4,3},{5,4},{6,5},{7,6},{8,7},{9,8},{10,9},{11,1... | collective-permute-start | bytes 393224 | tf_op jit(solution)/shard_map/ppermute | solution.py:18
  74.5 1.9 collective-permute-start.12
  76.5 7.5 %collective-permute-start.13 = (bf16[8,32,256]{2,1,0:T(8,128)(2,1)S(1)}, bf16[8,32,256]{2,1,0:T(8,128)(2,1)S(1)}, u32[]{:S(2)}, u32[]{:S(2)}) collective-permute-start(bf16[8,32,256]{2,1,0:T(8,128)(2,1)S(1)} %pad_maximum_fusion.6), channel_id=1, source_target_pairs={{1,0},{2,1},{3,2},{4,3},{5,4},{6,5},{7,6},{8,7},{9,8},{10,9},{11,1... | collective-permute-start | bytes 393224 | tf_op jit(solution)/shard_map/ppermute | solution.py:18
  84.0 1.9 collective-permute-start.16
  86.0 7.5 %collective-permute-start.17 = (bf16[8,32,256]{2,1,0:T(8,128)(2,1)S(1)}, bf16[8,32,256]{2,1,0:T(8,128)(2,1)S(1)}, u32[]{:S(2)}, u32[]{:S(2)}) collective-permute-start(bf16[8,32,256]{2,1,0:T(8,128)(2,1)S(1)} %pad_maximum_fusion.7), channel_id=1, source_target_pairs={{1,0},{2,1},{3,2},{4,3},{5,4},{6,5},{7,6},{8,7},{9,8},{10,9},{11,1... | collective-permute-start | bytes 393224 | tf_op jit(solution)/shard_map/ppermute | solution.py:18
  93.6 1.9 collective-permute-start.20
  95.7 7.5 %collective-permute-start.21 = (bf16[8,32,256]{2,1,0:T(8,128)(2,1)S(1)}, bf16[8,32,256]{2,1,0:T(8,128)(2,1)S(1)}, u32[]{:S(2)}, u32[]{:S(2)}) collective-permute-start(bf16[8,32,256]{2,1,0:T(8,128)(2,1)S(1)} %pad_maximum_fusion.8), channel_id=1, source_target_pairs={{1,0},{2,1},{3,2},{4,3},{5,4},{6,5},{7,6},{8,7},{9,8},{10,9},{11,1... | collective-permute-start | bytes 393224 | tf_op jit(solution)/shard_map/ppermute | solution.py:18
  103.2 1.9 collective-permute-start.2
  105.3 7.5 %collective-permute-start.3 = (bf16[8,32,256]{2,1,0:T(8,128)(2,1)S(1)}, bf16[8,32,256]{2,1,0:T(8,128)(2,1)S(1)}, u32[]{:S(2)}, u32[]{:S(2)}) collective-permute-start(bf16[8,32,256]{2,1,0:T(8,128)(2,1)S(1)} %constant_dynamic-update-slice_fusion), channel_id=1, source_target_pairs={{1,0},{2,1},{3,2},{4,3},{5,4},{6,5},{7,6},{8,7},{9,8},{10,9},{11,1... | collective-permute-start | bytes 393224 | tf_op jit(solution)/shard_map/ppermute | solution.py:18
  113.9 1.4 collective-permute-done.3
  117.1 1.3 fusion.46
  119.3 124.3 %all-reduce.4.cloned.1.call-done = f32[1024,256]{1,0:T(8,128)} async-done(((f32[1024,256]{1,0:T(8,128)}), f32[1024,256]{1,0:T(8,128)}) %all-reduce.4.cloned.1.call-update) | async-done | bytes 1048592 | tf_op jit(solution)/shard_map/psum | solution.py:114
  246.6 309.8 %all-reduce.6.cloned.1.call-done = f32[1024,256]{1,0:T(8,128)} async-done(((f32[1024,256]{1,0:T(8,128)}), f32[1024,256]{1,0:T(8,128)}) %all-reduce.6.cloned.1.call-update) | async-done | bytes 1048592 | tf_op jit(solution)/shard_map/psum | solution.py:114
  556.4 2.3 broadcast_multiply_fusion
  (117 shorter events, 13.5 us)
Async XLA Ops:
  7.2 0.8 copy-start
  7.2 15.8 %copy-start.1 = (bf16[4,256,256]{2,1,0:T(8,128)(2,1)S(1)}, bf16[4,256,256]{2,1,0:T(8,128)(2,1)}, u32[]{:S(2)}) copy-start(bf16[4,256,256]{2,1,0:T(8,128)(2,1)} %param.8) | copy-start | bytes 1572868
  7.2 236.4 %all-reduce.4.cloned.1.call-start = ((), (), s32[]{:S(2)}) async-start(), calls=%async_computation | async-start | bytes 2097152 | tf_op jit(solution)/shard_map/psum | solution.py:114
  9.1 30.2 %collective-permute-start.6 = (bf16[2,32,256]{2,1,0:T(8,128)(2,1)S(1)}, bf16[2,32,256]{2,1,0:T(8,128)(2,1)S(1)}, u32[]{:S(2)}, u32[]{:S(2)}) collective-permute-start(bf16[2,32,256]{2,1,0:T(8,128)(2,1)S(1)} %bitcast.278), channel_id=1, source_target_pairs={{0,32},{32,64},{64,96},{96,128},{128,160},{160,192},{192,224},{224... | collective-permute-start | bytes 98312 | tf_op jit(solution)/shard_map/ppermute | solution.py:16
  11.1 32.8 %collective-permute-start.7 = (bf16[2,32,256]{2,1,0:T(8,128)(2,1)S(1)}, bf16[2,32,256]{2,1,0:T(8,128)(2,1)S(1)}, u32[]{:S(2)}, u32[]{:S(2)}) collective-permute-start(bf16[2,32,256]{2,1,0:T(8,128)(2,1)S(1)} %bitcast.276), channel_id=1, source_target_pairs={{32,0},{64,32},{96,64},{128,96},{160,128},{192,160},{224,192},{256... | collective-permute-start | bytes 98312 | tf_op jit(solution)/shard_map/ppermute | solution.py:18
  18.7 11.6 %collective-permute-start.4 = (bf16[2,4,5,64]{3,1,2,0:T(4,128)(2,1)S(1)}, bf16[2,4,5,64]{3,1,2,0:T(4,128)(2,1)S(1)}, u32[]{:S(2)}, u32[]{:S(2)}) collective-permute-start(bf16[2,4,5,64]{3,1,2,0:T(4,128)(2,1)S(1)} %get-tuple-element.14), channel_id=1, source_target_pairs={{32,0},{64,32},{96,64},{128,96},{160,128},{192,160},{224,192},{256... | collective-permute-start | bytes 15368 | tf_op jit(solution)/shard_map/ppermute | solution.py:18
  20.6 14.0 %collective-permute-start.5 = (bf16[2,4,5,64]{3,1,2,0:T(4,128)(2,1)S(1)}, bf16[2,4,5,64]{3,1,2,0:T(4,128)(2,1)S(1)}, u32[]{:S(2)}, u32[]{:S(2)}) collective-permute-start(bf16[2,4,5,64]{3,1,2,0:T(4,128)(2,1)S(1)} %get-tuple-element.13), channel_id=1, source_target_pairs={{0,32},{32,64},{64,96},{96,128},{128,160},{160,192},{192,224},{224... | collective-permute-start | bytes 15368 | tf_op jit(solution)/shard_map/ppermute | solution.py:16
  23.2 22.6 %collective-permute-start.10 = (bf16[2,32,256]{2,1,0:T(8,128)(2,1)S(1)}, bf16[2,32,256]{2,1,0:T(8,128)(2,1)S(1)}, u32[]{:S(2)}, u32[]{:S(2)}) collective-permute-start(bf16[2,32,256]{2,1,0:T(8,128)(2,1)S(1)} %bitcast.281), channel_id=1, source_target_pairs={{0,32},{32,64},{64,96},{96,128},{128,160},{160,192},{192,224},{224... | collective-permute-start | bytes 98312 | tf_op jit(solution)/shard_map/ppermute | solution.py:16
  25.9 0.8 copy-start.7
  30.2 20.2 %collective-permute-start.11 = (bf16[2,32,256]{2,1,0:T(8,128)(2,1)S(1)}, bf16[2,32,256]{2,1,0:T(8,128)(2,1)S(1)}, u32[]{:S(2)}, u32[]{:S(2)}) collective-permute-start(bf16[2,32,256]{2,1,0:T(8,128)(2,1)S(1)} %bitcast.280), channel_id=1, source_target_pairs={{32,0},{64,32},{96,64},{128,96},{160,128},{192,160},{224,192},{256... | collective-permute-start | bytes 98312 | tf_op jit(solution)/shard_map/ppermute | solution.py:18
  34.6 23.9 %collective-permute-start.14 = (bf16[2,32,256]{2,1,0:T(8,128)(2,1)S(1)}, bf16[2,32,256]{2,1,0:T(8,128)(2,1)S(1)}, u32[]{:S(2)}, u32[]{:S(2)}) collective-permute-start(bf16[2,32,256]{2,1,0:T(8,128)(2,1)S(1)} %bitcast.279), channel_id=1, source_target_pairs={{0,32},{32,64},{64,96},{96,128},{128,160},{160,192},{192,224},{224... | collective-permute-start | bytes 98312 | tf_op jit(solution)/shard_map/ppermute | solution.py:16
  39.4 23.0 %collective-permute-start.15 = (bf16[2,32,256]{2,1,0:T(8,128)(2,1)S(1)}, bf16[2,32,256]{2,1,0:T(8,128)(2,1)S(1)}, u32[]{:S(2)}, u32[]{:S(2)}) collective-permute-start(bf16[2,32,256]{2,1,0:T(8,128)(2,1)S(1)} %bitcast.277), channel_id=1, source_target_pairs={{32,0},{64,32},{96,64},{128,96},{160,128},{192,160},{224,192},{256... | collective-permute-start | bytes 98312 | tf_op jit(solution)/shard_map/ppermute | solution.py:18
  43.9 32.6 %collective-permute-start.18 = (bf16[2,32,256]{2,1,0:T(8,128)(2,1)S(1)}, bf16[2,32,256]{2,1,0:T(8,128)(2,1)S(1)}, u32[]{:S(2)}, u32[]{:S(2)}) collective-permute-start(bf16[2,32,256]{2,1,0:T(8,128)(2,1)S(1)} %bitcast.275), channel_id=1, source_target_pairs={{0,32},{32,64},{64,96},{96,128},{128,160},{160,192},{192,224},{224... | collective-permute-start | bytes 98312 | tf_op jit(solution)/shard_map/ppermute | solution.py:16
  45.9 38.2 %collective-permute-start.19 = (bf16[2,32,256]{2,1,0:T(8,128)(2,1)S(1)}, bf16[2,32,256]{2,1,0:T(8,128)(2,1)S(1)}, u32[]{:S(2)}, u32[]{:S(2)}) collective-permute-start(bf16[2,32,256]{2,1,0:T(8,128)(2,1)S(1)} %bitcast.274), channel_id=1, source_target_pairs={{32,0},{64,32},{96,64},{128,96},{160,128},{192,160},{224,192},{256... | collective-permute-start | bytes 98312 | tf_op jit(solution)/shard_map/ppermute | solution.py:18
  50.4 6.1 %collective-permute-start = (bf16[2,32,256]{2,1,0:T(8,128)(2,1)S(1)}, bf16[2,32,256]{2,1,0:T(8,128)(2,1)S(1)}, u32[]{:S(2)}, u32[]{:S(2)}) collective-permute-start(bf16[2,32,256]{2,1,0:T(8,128)(2,1)S(1)} %get-tuple-element.12), channel_id=1, source_target_pairs={{0,32},{32,64},{64,96},{96,128},{128,160},{160,192},{192,224},{224... | collective-permute-start | bytes 98312 | tf_op jit(solution)/shard_map/ppermute | solution.py:16
  56.6 18.0 %collective-permute-start.1 = (bf16[2,32,256]{2,1,0:T(8,128)(2,1)S(1)}, bf16[2,32,256]{2,1,0:T(8,128)(2,1)S(1)}, u32[]{:S(2)}, u32[]{:S(2)}) collective-permute-start(bf16[2,32,256]{2,1,0:T(8,128)(2,1)S(1)} %get-tuple-element.11), channel_id=1, source_target_pairs={{32,0},{64,32},{96,64},{128,96},{160,128},{192,160},{224,192},{256... | collective-permute-start | bytes 98312 | tf_op jit(solution)/shard_map/ppermute | solution.py:18
  58.5 27.5 %collective-permute-start.8 = (bf16[8,32,256]{2,1,0:T(8,128)(2,1)S(1)}, bf16[8,32,256]{2,1,0:T(8,128)(2,1)S(1)}, u32[]{:S(2)}, u32[]{:S(2)}) collective-permute-start(bf16[8,32,256]{2,1,0:T(8,128)(2,1)S(1)} %pad_maximum_fusion.5), channel_id=1, source_target_pairs={{0,1},{1,2},{2,3},{3,4},{4,5},{5,6},{6,7},{7,8},{8,9},{9,10},{10,1... | collective-permute-start | bytes 393224 | tf_op jit(solution)/shard_map/ppermute | solution.py:16
  62.4 31.2 %collective-permute-start.9 = (bf16[8,32,256]{2,1,0:T(8,128)(2,1)S(1)}, bf16[8,32,256]{2,1,0:T(8,128)(2,1)S(1)}, u32[]{:S(2)}, u32[]{:S(2)}) collective-permute-start(bf16[8,32,256]{2,1,0:T(8,128)(2,1)S(1)} %pad_maximum_fusion.5), channel_id=1, source_target_pairs={{1,0},{2,1},{3,2},{4,3},{5,4},{6,5},{7,6},{8,7},{9,8},{10,9},{11,1... | collective-permute-start | bytes 393224 | tf_op jit(solution)/shard_map/ppermute | solution.py:18
  74.5 21.1 %collective-permute-start.12 = (bf16[8,32,256]{2,1,0:T(8,128)(2,1)S(1)}, bf16[8,32,256]{2,1,0:T(8,128)(2,1)S(1)}, u32[]{:S(2)}, u32[]{:S(2)}) collective-permute-start(bf16[8,32,256]{2,1,0:T(8,128)(2,1)S(1)} %pad_maximum_fusion.6), channel_id=1, source_target_pairs={{0,1},{1,2},{2,3},{3,4},{4,5},{5,6},{6,7},{7,8},{8,9},{9,10},{10,1... | collective-permute-start | bytes 393224 | tf_op jit(solution)/shard_map/ppermute | solution.py:16
  76.5 26.7 %collective-permute-start.13 = (bf16[8,32,256]{2,1,0:T(8,128)(2,1)S(1)}, bf16[8,32,256]{2,1,0:T(8,128)(2,1)S(1)}, u32[]{:S(2)}, u32[]{:S(2)}) collective-permute-start(bf16[8,32,256]{2,1,0:T(8,128)(2,1)S(1)} %pad_maximum_fusion.6), channel_id=1, source_target_pairs={{1,0},{2,1},{3,2},{4,3},{5,4},{6,5},{7,6},{8,7},{9,8},{10,9},{11,1... | collective-permute-start | bytes 393224 | tf_op jit(solution)/shard_map/ppermute | solution.py:18
  84.0 21.3 %collective-permute-start.16 = (bf16[8,32,256]{2,1,0:T(8,128)(2,1)S(1)}, bf16[8,32,256]{2,1,0:T(8,128)(2,1)S(1)}, u32[]{:S(2)}, u32[]{:S(2)}) collective-permute-start(bf16[8,32,256]{2,1,0:T(8,128)(2,1)S(1)} %pad_maximum_fusion.7), channel_id=1, source_target_pairs={{0,1},{1,2},{2,3},{3,4},{4,5},{5,6},{6,7},{7,8},{8,9},{9,10},{10,1... | collective-permute-start | bytes 393224 | tf_op jit(solution)/shard_map/ppermute | solution.py:16
  86.0 26.9 %collective-permute-start.17 = (bf16[8,32,256]{2,1,0:T(8,128)(2,1)S(1)}, bf16[8,32,256]{2,1,0:T(8,128)(2,1)S(1)}, u32[]{:S(2)}, u32[]{:S(2)}) collective-permute-start(bf16[8,32,256]{2,1,0:T(8,128)(2,1)S(1)} %pad_maximum_fusion.7), channel_id=1, source_target_pairs={{1,0},{2,1},{3,2},{4,3},{5,4},{6,5},{7,6},{8,7},{9,8},{10,9},{11,1... | collective-permute-start | bytes 393224 | tf_op jit(solution)/shard_map/ppermute | solution.py:18
  93.6 25.6 %collective-permute-start.20 = (bf16[8,32,256]{2,1,0:T(8,128)(2,1)S(1)}, bf16[8,32,256]{2,1,0:T(8,128)(2,1)S(1)}, u32[]{:S(2)}, u32[]{:S(2)}) collective-permute-start(bf16[8,32,256]{2,1,0:T(8,128)(2,1)S(1)} %pad_maximum_fusion.8), channel_id=1, source_target_pairs={{0,1},{1,2},{2,3},{3,4},{4,5},{5,6},{6,7},{7,8},{8,9},{9,10},{10,1... | collective-permute-start | bytes 393224 | tf_op jit(solution)/shard_map/ppermute | solution.py:16
  95.7 23.5 %collective-permute-start.21 = (bf16[8,32,256]{2,1,0:T(8,128)(2,1)S(1)}, bf16[8,32,256]{2,1,0:T(8,128)(2,1)S(1)}, u32[]{:S(2)}, u32[]{:S(2)}) collective-permute-start(bf16[8,32,256]{2,1,0:T(8,128)(2,1)S(1)} %pad_maximum_fusion.8), channel_id=1, source_target_pairs={{1,0},{2,1},{3,2},{4,3},{5,4},{6,5},{7,6},{8,7},{9,8},{10,9},{11,1... | collective-permute-start | bytes 393224 | tf_op jit(solution)/shard_map/ppermute | solution.py:18
  103.2 10.5 %collective-permute-start.2 = (bf16[8,32,256]{2,1,0:T(8,128)(2,1)S(1)}, bf16[8,32,256]{2,1,0:T(8,128)(2,1)S(1)}, u32[]{:S(2)}, u32[]{:S(2)}) collective-permute-start(bf16[8,32,256]{2,1,0:T(8,128)(2,1)S(1)} %constant_dynamic-update-slice_fusion), channel_id=1, source_target_pairs={{0,1},{1,2},{2,3},{3,4},{4,5},{5,6},{6,7},{7,8},{8,9},{9,10},{10,1... | collective-permute-start | bytes 393224 | tf_op jit(solution)/shard_map/ppermute | solution.py:16
  105.3 7.6 %copy-start.2 = (bf16[4,5,96,256]{3,2,1,0:T(8,128)(2,1)}, bf16[4,5,96,256]{3,2,1,0:T(8,128)(2,1)S(1)}, u32[]{:S(2)}) copy-start(bf16[4,5,96,256]{3,2,1,0:T(8,128)(2,1)S(1)} %fusion.17) | copy-start | bytes 2949124
  105.3 10.0 %collective-permute-start.3 = (bf16[8,32,256]{2,1,0:T(8,128)(2,1)S(1)}, bf16[8,32,256]{2,1,0:T(8,128)(2,1)S(1)}, u32[]{:S(2)}, u32[]{:S(2)}) collective-permute-start(bf16[8,32,256]{2,1,0:T(8,128)(2,1)S(1)} %constant_dynamic-update-slice_fusion), channel_id=1, source_target_pairs={{1,0},{2,1},{3,2},{4,3},{5,4},{6,5},{7,6},{8,7},{9,8},{10,9},{11,1... | collective-permute-start | bytes 393224 | tf_op jit(solution)/shard_map/ppermute | solution.py:18
  113.0 0.9 copy-start.4
  115.4 1.1 copy-start.6
  118.4 437.9 %all-reduce.6.cloned.1.call-start = ((), (), s32[]{:S(2)}) async-start(), calls=%async_computation.1 | async-start | bytes 2097152 | tf_op jit(solution)/shard_map/psum | solution.py:114
  243.6 1.2 copy-start.3
  244.0 1.3 copy-start.5
Sparse Core Ops, SparseCore 0:
  118.6 125.0 all-reduce.3
  246.5 309.8 all-reduce.5
